TPU v7x, 128 devices: a whole 4x4x4 slice. The times are simulated.
128 devices in a mesh: seq: 16 (over y_lo, x, core), cb: 8 (over y_hi, z).
Axes of the slice: x: 4, y: 4 (y_hi: 2, y_lo: 2; y = y_hi * 2 + y_lo), z: 4, core: 2. Of those that a mesh axis runs over, the one named last changes fastest.
Arguments:
- hidden: bfloat16 [2, 2048, 4096], P(None, 'seq'), may hold values from -6 to 6
- temporal_gain: float32 [4096], replicated, may hold values from 0.5 to 2
- temporal_qkv: bfloat16 [3, 4096, 2048], P(None, None, 'cb'), may hold values from -10 to 10
- temporal_out: bfloat16 [2048, 4096], P('cb'), may hold values from -0.125 to 0.125
- codebook_ids: int32 [2, 2048, 8], P(None, 'seq', 'cb'), may hold values from 0 to 2047
- embedding: bfloat16 [8, 2048, 1024], P('cb'), may hold values from -6 to 6
- input_weight: bfloat16 [8, 4096, 1024], P('cb', 'seq'), may hold values from -0.09375 to 0.09375
- depth_gain: float32 [8, 1024], P('cb'), may hold values from 0.5 to 2
- depth_qkv: bfloat16 [8, 3, 1024, 1024], P('cb'), may hold values from -10 to 10
- depth_out: bfloat16 [8, 1024, 1024], P('cb'), may hold values from -0.1875 to 0.1875
Outputs:
- temporal: bfloat16 [2, 2048, 4096], P(None, 'seq')
- depth: bfloat16 [2, 2048, 8, 1024], P(None, 'seq', 'cb')
All inputs are finite; a program needn't handle non-finite values.
Results may differ from a plain program's by a relative error of at most 0.017.
Values may be sent and summed in bfloat16 or wider, within the bound.
A program may use at most 128 MiB of HBM per device.

v0:
```python
import jax
import jax.numpy as jnp
from jax import lax
from jax.sharding import PartitionSpec as P

HD = 128
DW = 1024
DH = 16
DHD = 64


def normalize(values, scale):
    mean_sq = jnp.mean(values * values, axis=-1, keepdims=True)
    return values * lax.rsqrt(mean_sq + 1e-05) * scale


def shards(
    hidden,
    temporal_gain,
    temporal_qkv,
    temporal_out,
    codebook_ids,
    embedding,
    input_weight,
    depth_gain,
    depth_qkv,
    depth_out,
):
    seq_count, frames, width = hidden.shape
    head_cols = temporal_qkv.shape[2]
    head_count = head_cols // HD
    row_count = seq_count * frames
    hidden_f = hidden.astype(jnp.float32)
    normed = normalize(hidden_f, temporal_gain).astype(jnp.bfloat16).reshape(row_count, width)
    projected = []
    for which in range(3):
        part_rows = jnp.dot(normed, temporal_qkv[which], preferred_element_type=jnp.float32).astype(
            jnp.bfloat16
        )
        projected.append(part_rows.reshape(seq_count, frames, head_count, HD))
    queries = projected[0]
    query_pos = lax.axis_index("seq") * frames + jnp.arange(frames, dtype=jnp.int32)
    temporal_scale = 1.0 / jnp.sqrt(jnp.float32(HD))
    highest = jnp.full((seq_count, head_count, frames), -1e30, jnp.float32)
    key_piece = lax.all_gather(projected[1], "seq", axis=1, tiled=True)
    value_piece = lax.all_gather(projected[2], "seq", axis=1, tiled=True)
    count = key_piece.shape[1]
    scores = (
        jnp.einsum("sqhd,skhd->shqk", queries, key_piece, preferred_element_type=jnp.float32)
        * temporal_scale
    )
    key_pos = jnp.arange(count, dtype=jnp.int32)
    allowed = (key_pos[None, :] <= query_pos[:, None])[None, None]
    scores = jnp.where(allowed, scores, -1e30)
    new_high = jnp.maximum(highest, jnp.max(scores, axis=-1))
    weights = jnp.where(allowed, jnp.exp(scores - new_high[..., None]), 0.0)
    totals = jnp.sum(weights, axis=-1)
    update = jnp.einsum(
        "shqk,skhd->sqhd",
        weights.astype(jnp.bfloat16),
        value_piece,
        preferred_element_type=jnp.float32,
    )
    gathered = update
    highest, totals, gathered = (new_high, totals, gathered)
    mixed = (
        (gathered / totals.transpose(0, 2, 1)[..., None])
        .astype(jnp.bfloat16)
        .reshape(row_count, head_cols)
    )
    term = jnp.dot(mixed, temporal_out, preferred_element_type=jnp.float32)
    summed = lax.psum(term.astype(jnp.bfloat16), "cb").astype(jnp.float32)
    temporal = (hidden_f.reshape(row_count, width) + summed).astype(jnp.bfloat16)
    projected_in = jnp.dot(
        temporal,
        lax.all_gather(input_weight, "seq", axis=1, tiled=True)[0],
        preferred_element_type=jnp.float32,
    )
    entry = jnp.take(embedding[0], codebook_ids.reshape(row_count), axis=0).astype(jnp.float32)
    stream = (projected_in + entry).astype(jnp.bfloat16)
    depth_normed = normalize(stream.astype(jnp.float32), depth_gain[0]).astype(jnp.bfloat16)
    book_query = jnp.dot(depth_normed, depth_qkv[0, 0], preferred_element_type=jnp.float32).astype(
        jnp.bfloat16
    )
    book_key = jnp.dot(depth_normed, depth_qkv[0, 1], preferred_element_type=jnp.float32).astype(
        jnp.bfloat16
    )
    book_value = jnp.dot(depth_normed, depth_qkv[0, 2], preferred_element_type=jnp.float32).astype(
        jnp.bfloat16
    )
    depth_scale = 1.0 / jnp.sqrt(jnp.float32(DHD))
    my_book = lax.axis_index("cb")
    query_heads = book_query.reshape(row_count, DH, DHD)
    highest_b = jnp.full((row_count, DH), -1e30, jnp.float32)
    key_piece = lax.all_gather(book_key[None], "cb", axis=0, tiled=True)
    value_piece = lax.all_gather(book_value[None], "cb", axis=0, tiled=True)
    count = key_piece.shape[0]
    key_heads = key_piece.reshape(count, row_count, DH, DHD)
    value_heads = value_piece.reshape(count, row_count, DH, DHD)
    scores = (
        jnp.einsum("rhd,jrhd->rhj", query_heads, key_heads, preferred_element_type=jnp.float32)
        * depth_scale
    )
    permitted = (jnp.arange(count, dtype=jnp.int32) <= my_book)[None, None, :]
    scores = jnp.where(permitted, scores, -1e30)
    new_high = jnp.maximum(highest_b, jnp.max(scores, axis=-1))
    weights = jnp.where(permitted, jnp.exp(scores - new_high[..., None]), 0.0)
    totals_b = jnp.sum(weights, axis=-1)
    update = jnp.einsum(
        "rhj,jrhd->rhd",
        weights.astype(jnp.bfloat16),
        value_heads,
        preferred_element_type=jnp.float32,
    )
    highest_b, totals_b, gathered_b = (new_high, totals_b, update)
    book_mixed = (gathered_b / totals_b[..., None]).astype(jnp.bfloat16).reshape(row_count, DW)
    depth = (
        jnp.dot(book_mixed, depth_out[0], preferred_element_type=jnp.float32)
        + stream.astype(jnp.float32)
    ).astype(jnp.bfloat16)
    return (temporal.reshape(seq_count, frames, width), depth.reshape(seq_count, frames, 1, DW))


def solution(mesh):
    placed = (
        P(None, "seq", None),
        P(),
        P(None, None, "cb"),
        P("cb", None),
        P(None, "seq", "cb"),
        P("cb", None, None),
        P("cb", "seq", None),
        P("cb", None),
        P("cb", None, None, None),
        P("cb", None, None),
    )
    return jax.shard_map(
        shards,
        mesh=mesh,
        in_specs=placed,
        out_specs=(P(None, "seq", None), P(None, "seq", "cb", None)),
        check_vma=False,
    )
```

profile of v0, /device:TPU:126, one launch (start us, length us, event | category | flops | bytes accessed | tf_op | source)
XLA Modules:
  0.0 413.9 jit_solution(1029900267491474171)
XLA Ops:
  7.2 2.2 multiply_reduce_fusion.2
  9.5 2.3 multiply_convert_fusion
  13.1 2.3 fusion.58
  16.3 2.9 fusion.52
  20.1 2.9 fusion.55
  23.3 26.3 %all-gather.10.cloned.1.call-done = bf16[2,2048,2,128]{3,1,2,0:T(8,128)(2,1)} async-done(((bf16[2,128,2,128]{3,1,2,0:T(8,128)(2,1)}), bf16[2,2048,2,128]{3,1,2,0:T(8,128)(2,1)}) %all-gather.10.cloned.1.call-update) | async-done | bytes 2097168 | tf_op jit(solution)/shard_map/all_gather | solution.py:45
  49.6 2.6 fusion.3
  55.4 33.8 %all-gather.8.cloned.1.call-done = bf16[2,2048,2,128]{1,3,2,0:T(8,128)(2,1)} async-done(((bf16[2,128,2,128]{1,3,2,0:T(8,128)(2,1)}), bf16[2,2048,2,128]{1,3,2,0:T(8,128)(2,1)}) %all-gather.8.cloned.1.call-update) | async-done | bytes 2097168 | tf_op jit(solution)/shard_map/all_gather | solution.py:46
  89.2 4.1 fusion.64
  96.4 4.3 %gather_fusion = bf16[256,1024]{1,0:T(8,128)(2,1)S(1)} fusion(bf16[2048,1024]{1,0:T(8,128)(2,1)} %bitcast.102, s32[1024]{0:T(1024)S(1)} %pad_clamp_fusion), kind=kCustom, calls=%fused_computation | custom fusion | bytes 1049600 | tf_op jit(solution)/shard_map/jit(_take)/gather | solution.py:79
  100.7 86.9 %all-reduce.2.cloned.1.call-done = bf16[256,4096]{1,0:T(8,128)(2,1)} async-done(((bf16[256,4096]{1,0:T(8,128)(2,1)}), bf16[256,4096]{1,0:T(8,128)(2,1)}) %all-reduce.2.cloned.1.call-update) | async-done | bytes 2097168 | tf_op jit(solution)/shard_map/psum | solution.py:72
  187.6 3.7 fusion.2
  191.3 50.6 %all-gather.12.cloned.1.call-done = bf16[1,4096,1024]{2,1,0:T(8,128)(2,1)} async-done(((bf16[1,256,1024]{2,1,0:T(8,128)(2,1)}), bf16[1,4096,1024]{2,1,0:T(8,128)(2,1)}) %all-gather.12.cloned.1.call-update) | async-done | bytes 8388624 | tf_op jit(solution)/shard_map/all_gather | solution.py:76
  241.9 6.5 %fusion.67 = (f32[256]{0:T(256)S(1)}, bf16[256,1024]{1,0:T(8,128)(2,1)S(1)}) fusion(bf16[256,1024]{1,0:T(8,128)(2,1)S(1)} %gather_fusion, pred[256]{0:T(512)(128)(4,1)S(1)} %compare_and_fusion, bf16[256,4096]{1,0:T(8,128)(2,1)} %fusion.2, bf16[1,4096,1024]{2,1,0:T(8,128)(2,1)} %all-gather.12.cloned.1.call-done), kind=kOutput, calls=%fused_computation.52 | convolution fusion | flops 2149318400 | bytes 11535616 | tf_op jit(solution)/shard_map/dot_general | solution.py:74
  248.4 3.1 fusion.43
  251.8 3.2 fusion.46
  255.0 2.4 fusion.40
  257.7 63.3 %all-gather.14.cloned.1.call-done = bf16[2048,1024]{1,0:T(8,128)(2,1)} async-done(((bf16[256,1024]{1,0:T(8,128)(2,1)}), bf16[2048,1024]{1,0:T(8,128)(2,1)}) %all-gather.14.cloned.1.call-update) | async-done | bytes 4194320 | tf_op jit(solution)/shard_map/all_gather | solution.py:95
  321.0 6.5 %copy.29 = bf16[2048,1024]{0,1:T(8,128)(2,1)} copy(bf16[2048,1024]{1,0:T(8,128)(2,1)} %all-gather.14.cloned.1.call-done) | data formatting | bytes 8388608 | tf_op jit(solution)/shard_map/all_gather | solution.py:95
  327.5 3.7 copy.47
  332.4 60.2 %all-gather.16.cloned.1.call-done = bf16[2048,1024]{1,0:T(8,128)(2,1)} async-done(((bf16[256,1024]{1,0:T(8,128)(2,1)}), bf16[2048,1024]{1,0:T(8,128)(2,1)}) %all-gather.16.cloned.1.call-update) | async-done | bytes 4194320 | tf_op jit(solution)/shard_map/all_gather | solution.py:96
  392.6 6.5 %copy.30 = bf16[2048,1024]{0,1:T(8,128)(2,1)} copy(bf16[2048,1024]{1,0:T(8,128)(2,1)} %all-gather.16.cloned.1.call-done) | data formatting | bytes 8388608 | tf_op jit(solution)/shard_map/all_gather | solution.py:96
  399.1 3.7 copy.48
  402.8 2.6 multiply_reduce_fusion
  (53 shorter events, 12.9 us)
Async XLA Ops:
  7.2 86.3 %copy-start = (bf16[256,4096]{1,0:T(8,128)(2,1)S(1)}, bf16[256,4096]{1,0:T(8,128)(2,1)}, u32[]{:S(2)}) copy-start(bf16[256,4096]{1,0:T(8,128)(2,1)} %param.13) | copy-start | bytes 6291460
  7.2 42.4 %all-gather.10.cloned.1.call-start = ((), (), s32[]{:S(2)}) async-start(), calls=%async_computation.1 | async-start | bytes 2228224 | tf_op jit(solution)/shard_map/all_gather | solution.py:45
  11.8 1.3 copy-start.5
  16.2 73.0 %all-gather.8.cloned.1.call-start = ((), (), s32[]{:S(2)}) async-start(), calls=%async_computation | async-start | bytes 2228224 | tf_op jit(solution)/shard_map/all_gather | solution.py:46
  20.0 167.6 %all-reduce.2.cloned.1.call-start = ((), (), s32[]{:S(2)}) async-start(), calls=%async_computation.2 | async-start | bytes 4194304 | tf_op jit(solution)/shard_map/psum | solution.py:72
  52.2 1.9 copy-start.3
  93.4 3.0 copy-start.6
  95.6 92.1 %copy-start.2 = (bf16[2,128,4096]{2,1,0:T(8,128)(2,1)S(1)}, bf16[2,128,4096]{2,1,0:T(8,128)(2,1)}, u32[]{:S(2)}) copy-start(bf16[2,128,4096]{2,1,0:T(8,128)(2,1)} %param.10) | copy-start | bytes 6291460
  95.6 146.3 %all-gather.12.cloned.1.call-start = ((), (), s32[]{:S(2)}) async-start(), calls=%async_computation.3 | async-start | bytes 8912896 | tf_op jit(solution)/shard_map/all_gather | solution.py:76
  96.2 224.9 %all-gather.14.cloned.1.call-start = ((), (), s32[]{:S(2)}) async-start(), calls=%async_computation.4 | async-start | bytes 4718592 | tf_op jit(solution)/shard_map/all_gather | solution.py:95
  191.3 57.1 %copy-start.7 = (f32[1,1024]{1,0:T(1,128)S(1)}, f32[1,1024]{1,0:T(1,128)}, u32[]{:S(2)}) copy-start(f32[1,1024]{1,0:T(1,128)} %param.17) | copy-start | bytes 12292
  251.6 141.0 %all-gather.16.cloned.1.call-start = ((), (), s32[]{:S(2)}) async-start(), calls=%async_computation.5 | async-start | bytes 4718592 | tf_op jit(solution)/shard_map/all_gather | solution.py:96
  402.8 2.8 copy-start.4
  402.8 4.3 %copy-start.1 = (bf16[256,4096]{1,0:T(8,128)(2,1)S(1)}, bf16[256,4096]{1,0:T(8,128)(2,1)}, u32[]{:S(2)}) copy-start(bf16[256,4096]{1,0:T(8,128)(2,1)} %param.13) | copy-start | bytes 6291460
Sparse Core Ops, SparseCore 0:
  16.3 33.2 all-gather.9
  51.8 37.4 all-gather.7
  95.7 91.8 all-reduce.1
  189.2 52.6 all-gather.11
  251.7 69.3 all-gather.13
  323.3 69.2 all-gather.15
where the time goes:
time: 420 us; the launch traced here: 414 us
  waiting for transfers between devices  322 us (77%)
  matrix products  33.6 us (8%)
  local copies, waits for them, and re-layouts  29.8 us (7%)
  between operations  14.4 us (3%)
  other arithmetic  13.8 us (3%)
    psum x1, waiting for transfers between devices, shards(): summed = lax.psum(term.astype(jnp.bfloat16), 'cb').astype(jnp.float32)  86.9 us
    all_gather x1, waiting for transfers between devices, shards(): key_piece = lax.all_gather(book_key[None], 'cb', axis=0, tiled=True)  63.3 us
    all_gather x1, waiting for transfers between devices, shards(): value_piece = lax.all_gather(book_value[None], 'cb', axis=0, tiled=True)  60.2 us
    all_gather x1, waiting for transfers between devices, shards(): lax.all_gather(input_weight, 'seq', axis=1, tiled=True)[0]  50.6 us
    all_gather x1, waiting for transfers between devices, shards(): value_piece = lax.all_gather(projected[2], 'seq', axis=1, tiled=True)  33.8 us
    all_gather x1, waiting for transfers between devices, shards(): key_piece = lax.all_gather(projected[1], 'seq', axis=1, tiled=True)  26.3 us
    unnamed x18, local copies, waits for them, and re-layouts  10.6 us
  transfers between devices with their start and end apart: 6, of which 6 were waited for; matrix products, arithmetic and copies ran while one was open for 9% of the time, Pallas kernels for 0%

commit v1 on v0

v1 whole, which is shorter than its diff:
```python
import jax
import jax.numpy as jnp
from jax import lax
from jax.experimental import pallas as pl
from jax.experimental.pallas import tpu as pltpu
from jax.sharding import PartitionSpec as P

MESH = pl.DeviceIdType.MESH
F32, BF16 = jnp.float32, jnp.bfloat16
EPS = 1e-05
CB_STEPS = [(0, 1), (0, 3), (0, 2), (1, 0), (1, 1), (1, 3), (1, 2)]
SEQ_STEPS = [(0, 1), (0, 3), (1, 0), (0, 2), (1, 1), (1, 3), (1, 2)]


def dot(a, b):
    return jnp.dot(a, b, preferred_element_type=F32)


def body(
    hidden, gain, qkv_w, out_w, ids, embedding, in_w, depth_gain, depth_qkv, depth_out,
    temporal_out, depth_res,
    hid, normed, wq, kvq, kv, qs, att, mix, wo, tb, win, emb, dw, do, acc, stream, dnorm, dsend, drecv, bsend, brecv,
    local_sem, kv_send, kv_recv, kvf_send, kvf_recv, q_send, q_recv, r_send, r_recv, m_send, m_recv,
    wo_send, wo_recv, t_send, t_recv, to_sem, wi_send, wi_recv, wf_send, wf_recv, d_send, d_recv, b_send, b_recv,
):
    s = lax.axis_index("seq")
    c = lax.axis_index("cb")
    yl, x, co = s // 8, (s // 2) % 4, s % 2
    yh, z = c // 4, c % 4
    rank = yl * 2 + co

    def cb_at(step, sign=1):
        return ((yh + step[0]) % 2) * 4 + (z + sign * step[1] + 4) % 4

    def seq_at(step, sign=1):
        return ((yl + step[0]) % 2) * 8 + ((x + sign * step[1] + 4) % 4) * 2 + co

    sibling = s + 1 - 2 * co

    def remote(src, dst, send, recv, device):
        return pltpu.make_async_remote_copy(
            src_ref=src, dst_ref=dst, send_sem=send, recv_sem=recv, device_id=device, device_id_type=MESH
        )

    def arrive(ref, sem):
        pltpu.make_async_copy(ref, ref, sem).wait()

    pending = []

    def send(copy, when=None):
        if when is None:
            copy.start()
        else:
            pl.when(when)(copy.start)
        pending.append((copy, when))

    barrier = pltpu.get_barrier_semaphore()
    for step in CB_STEPS:
        pl.semaphore_signal(barrier, inc=1, device_id=(s, cb_at(step)), device_id_type=MESH)
    for step in SEQ_STEPS:
        pl.semaphore_signal(barrier, inc=1, device_id=(seq_at(step), c), device_id_type=MESH)
        other = seq_at(step) + 1 - 2 * co
        pl.semaphore_signal(barrier, inc=1, device_id=(other, c), device_id_type=MESH)
    pl.semaphore_signal(barrier, inc=1, device_id=(sibling, c), device_id_type=MESH)

    loads = [
        pltpu.make_async_copy(hidden, hid, local_sem.at[0]),
        pltpu.make_async_copy(qkv_w.at[1], wq.at[1], local_sem.at[1]),
        pltpu.make_async_copy(qkv_w.at[2], wq.at[2], local_sem.at[2]),
        pltpu.make_async_copy(qkv_w.at[0], wq.at[0], local_sem.at[3]),
        pltpu.make_async_copy(out_w.at[:, pl.ds(pl.multiple_of(c * 512, 512), 512)], wo.at[c], local_sem.at[4]),
        pltpu.make_async_copy(in_w, win.at[s], local_sem.at[5]),
        pltpu.make_async_copy(embedding, emb, local_sem.at[6]),
        pltpu.make_async_copy(depth_qkv, dw, local_sem.at[7]),
        pltpu.make_async_copy(depth_out, do, local_sem.at[8]),
    ]
    for copy in loads:
        copy.start()

    loads[0].wait()

    @pl.loop(0, 16)
    def _(i):
        rows = pl.ds(pl.multiple_of(i * 16, 16), 16)
        values = hid[rows, :].astype(F32)
        mean_sq = jnp.mean(values * values, axis=-1, keepdims=True)
        normed[rows, :] = (values * lax.rsqrt(mean_sq + EPS) * gain[...]).astype(BF16)

    def project(which, slot):
        loads[{1: 1, 2: 2, 0: 3}[which]].wait()
        res = dot(normed[...], wq[which]).astype(BF16)
        for g in range(4):
            b, h = g // 2, g % 2
            kvq[g, slot] = res[b * 128 : (b + 1) * 128, h * 128 : (h + 1) * 128]

    project(1, 0)
    project(2, 1)
    pl.semaphore_wait(barrier, 22)

    for i, step in enumerate(SEQ_STEPS):
        to = seq_at(step)
        g = (to // 2) % 4
        send(remote(kvq.at[g, pl.ds(0, 2)], kv.at[s], kv_send.at[i], kv_recv.at[i], (to, c)))
    kv[s] = kvq[x, 0:2]
    send(remote(kv.at[s], kv.at[s], kvf_send.at[7], kvf_recv.at[7], (sibling, c)))

    for i, step in enumerate(CB_STEPS):
        to = cb_at(step)
        columns = pl.ds(pl.multiple_of(to * 512, 512), 512)
        send(remote(out_w.at[:, columns], wo.at[c], wo_send.at[i], wo_recv.at[i], (s, to)))

    project(0, 2)
    turn = s % 8
    owner = jnp.where(turn < 4, turn, 7 - turn)
    strip = s // 4
    for dx in range(4):
        g = (x + dx) % 4
        to = (owner // 2) * 8 + g * 2 + owner % 2
        copy = remote(kvq.at[g, 2], qs.at[strip], q_send.at[dx], q_recv.at[strip], (to, c))
        send(copy, None if dx else owner != rank)

    @pl.when(owner == rank)
    def _():
        qs[strip] = kvq[x, 2]

    send(remote(in_w, win.at[s], wi_send.at[0], wi_recv.at[0], (seq_at((1, 0)), c)))
    for i in (1, 3, 2):
        send(remote(in_w, win.at[s], wi_send.at[i], wi_recv.at[i], (seq_at((0, i)), c)))
    send(remote(in_w, win.at[s], wf_send.at[0], wf_recv.at[0], (sibling, c)))

    for i, step in enumerate(SEQ_STEPS):
        source = seq_at(step, -1)
        arrive(kv.at[source], kv_recv.at[i])
        send(remote(kv.at[source], kv.at[source], kvf_send.at[i], kvf_recv.at[i], (sibling, c)))
    arrive(kv.at[sibling], kvf_recv.at[7])
    for i, step in enumerate(SEQ_STEPS):
        source = seq_at(step, -1) + 1 - 2 * co
        arrive(kv.at[source], kvf_recv.at[i])

    for k in range(4):
        block = 4 * k + (rank if k % 2 == 0 else 3 - rank)

        @pl.when(block != s)
        def _():
            arrive(qs.at[k], q_recv.at[k])

        n = 4 * (k + 1)
        keys = kv[0:n, 0].reshape(n * 128, 128)
        values = kv[0:n, 1].reshape(n * 128, 128)
        scores = lax.dot_general(qs[k], keys, (((1,), (1,)), ((), ())), preferred_element_type=F32)
        row = lax.broadcasted_iota(jnp.int32, scores.shape, 0) + block * 128
        col = lax.broadcasted_iota(jnp.int32, scores.shape, 1)
        allowed = col <= row
        scores = jnp.where(allowed, scores * (128.0**-0.5), -1e30)
        weights = jnp.where(allowed, jnp.exp(scores - jnp.max(scores, axis=-1, keepdims=True)), 0.0)
        totals = jnp.sum(weights, axis=-1, keepdims=True)
        att[k] = (dot(weights.astype(BF16), values) / totals).astype(BF16)
        send(remote(att.at[k], mix.at[c, x], r_send.at[k], r_recv.at[x], (block, c)), block != s)

        @pl.when(block == s)
        def _():
            mix[c, x] = att[k]

    across = seq_at((1, 0))
    arrive(win.at[across], wi_recv.at[0])
    for i in (1, 3, 2):
        send(remote(win.at[across], win.at[across], wi_send.at[3 + i], wi_recv.at[3 + i], (seq_at((0, i)), c)))
    send(remote(win.at[across], win.at[across], wf_send.at[1], wf_recv.at[1], (sibling, c)))

    for g in range(4):
        @pl.when(jnp.logical_or(g != x, owner != rank))
        def _():
            arrive(mix.at[c, g], r_recv.at[g])

    for i, step in enumerate(CB_STEPS):
        send(remote(mix.at[c], mix.at[c], m_send.at[i], m_recv.at[i], (s, cb_at(step))))

    def group_term(group):
        top = jnp.concatenate([mix[group, 0], mix[group, 1]], axis=1)
        low = jnp.concatenate([mix[group, 2], mix[group, 3]], axis=1)
        return dot(jnp.concatenate([top, low], axis=0), wo[group])

    loads[4].wait()
    summed = group_term(c)
    for i, step in enumerate(CB_STEPS):
        group = cb_at(step, -1)
        arrive(wo.at[group], wo_recv.at[i])
        arrive(mix.at[group], m_recv.at[i])
        summed = summed + group_term(group)
    mine = pl.ds(pl.multiple_of(c * 512, 512), 512)
    tb[c] = (hid[:, mine].astype(F32) + summed).astype(BF16)
    for i, step in enumerate(CB_STEPS):
        send(remote(tb.at[c], tb.at[c], t_send.at[i], t_recv.at[i], (s, cb_at(step))))
    stores = []

    def store(index, group):
        columns = pl.ds(pl.multiple_of(group * 512, 512), 512)
        copy = pltpu.make_async_copy(tb.at[group], temporal_out.at[:, columns], to_sem.at[index])
        copy.start()
        stores.append(copy)

    store(7, c)

    loads[6].wait()
    picks = []
    for b in range(2):
        picks.append(jnp.broadcast_to(ids[b : b + 1, :], (128, 128)).T)
    acc[...] = jnp.zeros_like(acc)

    @pl.loop(0, 8)
    def _(k):
        lane = lax.broadcasted_iota(jnp.int32, (128, 128), 1) + k * 256
        hot = [
            jnp.concatenate([jnp.where(pick == lane + 128 * j, 1.0, 0.0).astype(BF16) for j in range(2)], axis=1)
            for pick in picks
        ]
        acc[...] += dot(jnp.concatenate(hot, axis=0), emb[pl.ds(pl.multiple_of(k * 256, 256), 256), :])

    loads[5].wait()
    for i in (1, 3, 2):
        source = seq_at((0, i), -1)
        arrive(win.at[source], wi_recv.at[i])
        send(remote(win.at[source], win.at[source], wf_send.at[1 + i], wf_recv.at[1 + i], (sibling, c)))
    for i in (1, 3, 2):
        source = seq_at((1, i), -1)
        arrive(win.at[source], wi_recv.at[3 + i])
        send(remote(win.at[source], win.at[source], wf_send.at[4 + i], wf_recv.at[4 + i], (sibling, c)))
    twin = 1 - 2 * co
    arrive(win.at[sibling], wf_recv.at[0])
    arrive(win.at[across + twin], wf_recv.at[1])
    for i in (1, 3, 2):
        arrive(win.at[seq_at((0, i), -1) + twin], wf_recv.at[1 + i])
        arrive(win.at[seq_at((1, i), -1) + twin], wf_recv.at[4 + i])

    def add_block(group):
        rows = jnp.concatenate([win[2 * group], win[2 * group + 1]], axis=0)
        acc[...] += dot(tb[group], rows)

    add_block(c)
    for i, step in enumerate(CB_STEPS):
        group = cb_at(step, -1)
        arrive(tb.at[group], t_recv.at[i])
        store(i, group)
        add_block(group)

    @pl.loop(0, 8)
    def _(i):
        rows = pl.ds(pl.multiple_of(i * 32, 32), 32)
        rounded = acc[rows, :].astype(BF16)
        stream[rows, :] = rounded
        values = rounded.astype(F32)
        mean_sq = jnp.mean(values * values, axis=-1, keepdims=True)
        dnorm[rows, :] = (values * lax.rsqrt(mean_sq + EPS) * depth_gain[...]).astype(BF16)

    loads[7].wait()
    for i in (2, 1, 3, 0):
        pair = (c // 2 + i) % 4
        columns = pl.ds(pl.multiple_of(pair * 256, 256), 256)
        for which in range(3):
            res = dot(dnorm[...], dw[which, :, columns]).astype(BF16)
            dsend[2 * pair, which] = res[:, 0:128]
            dsend[2 * pair + 1, which] = res[:, 128:256]
        if i:
            for j in range(2):
                to = 2 * pair + j
                send(remote(dsend.at[to], drecv.at[c], d_send.at[2 * i + j], d_recv.at[c], (s, to)))
        else:
            to = c + 1 - 2 * (c % 2)
            send(remote(dsend.at[to], drecv.at[c], d_send.at[0], d_recv.at[c], (s, to)))
            drecv[c] = dsend[c]

    for book in range(8):
        @pl.when(book != c)
        def _():
            arrive(drecv.at[book], d_recv.at[book])

    half_a = lax.broadcasted_iota(jnp.int32, (256, 128), 0) % 128 // 64
    half_b = lax.broadcasted_iota(jnp.int32, (256, 128), 1) // 64
    same_head = jnp.where(half_a == half_b, 1.0, 0.0).astype(BF16)
    size = 64
    for book in range(8):
        @pl.loop(0, 256 // size)
        def _(i):
            rows = pl.ds(pl.multiple_of(i * size, size), size)
            query = drecv[book, 0, rows, :].astype(F32)
            parts = []
            for j in range(book + 1):
                prod = query * drecv[j, 1, rows, :].astype(F32)
                high = prod.astype(BF16)
                low = (prod - high.astype(F32)).astype(BF16)
                parts.append(jnp.concatenate([high, low], axis=1))
            scores = dot(jnp.concatenate(parts, axis=0), same_head)
            scores = [scores[j * size : (j + 1) * size] for j in range(book + 1)]
            highest = scores[0]
            for j in range(1, book + 1):
                highest = jnp.maximum(highest, scores[j])
            totals = jnp.zeros((size, 128), F32)
            mixed = jnp.zeros((size, 128), F32)
            for j in range(book + 1):
                weight = jnp.exp((scores[j] - highest) * 0.125)
                totals = totals + weight
                mixed = mixed + weight.astype(BF16).astype(F32) * drecv[j, 2, rows, :].astype(F32)
            bsend[book, rows, :] = (mixed / totals).astype(BF16)

        send(remote(bsend.at[book], brecv.at[c], b_send.at[book], b_recv.at[c], (s, book)), book != c)

        @pl.when(book == c)
        def _():
            brecv[c] = bsend[book]

    loads[8].wait()
    for head in range(8):
        @pl.when(head != c)
        def _():
            arrive(brecv.at[head], b_recv.at[head])

    book_mixed = jnp.concatenate([brecv[head] for head in range(8)], axis=1)
    depth_res[...] = (dot(book_mixed, do[...]) + stream[...].astype(F32)).astype(BF16)

    for copy in stores:
        copy.wait()
    for copy, when in pending:
        if when is None:
            copy.wait_send()
        else:
            pl.when(when)(copy.wait_send)


def shards(hidden, gain, qkv_w, out_w, ids, embedding, in_w, depth_gain, depth_qkv, depth_out):
    anywhere = pl.BlockSpec(memory_space=pl.ANY)
    vmem = pl.BlockSpec(memory_space=pltpu.VMEM)
    dma = pltpu.SemaphoreType.DMA
    temporal, depth = pl.pallas_call(
        body,
        out_shape=(jax.ShapeDtypeStruct((256, 4096), BF16), jax.ShapeDtypeStruct((256, 1024), BF16)),
        in_specs=[anywhere, vmem, anywhere, anywhere, vmem, anywhere, anywhere, vmem, anywhere, anywhere],
        out_specs=(anywhere, vmem),
        scratch_shapes=[
            pltpu.VMEM((256, 4096), BF16),
            pltpu.VMEM((256, 4096), BF16),
            pltpu.VMEM((3, 4096, 256), BF16),
            pltpu.VMEM((4, 3, 128, 128), BF16),
            pltpu.VMEM((16, 2, 128, 128), BF16),
            pltpu.VMEM((4, 128, 128), BF16),
            pltpu.VMEM((4, 128, 128), BF16),
            pltpu.VMEM((8, 4, 128, 128), BF16),
            pltpu.VMEM((8, 256, 512), BF16),
            pltpu.VMEM((8, 256, 512), BF16),
            pltpu.VMEM((16, 256, 1024), BF16),
            pltpu.VMEM((2048, 1024), BF16),
            pltpu.VMEM((3, 1024, 1024), BF16),
            pltpu.VMEM((1024, 1024), BF16),
            pltpu.VMEM((256, 1024), F32),
            pltpu.VMEM((256, 1024), BF16),
            pltpu.VMEM((256, 1024), BF16),
            pltpu.VMEM((8, 3, 256, 128), BF16),
            pltpu.VMEM((8, 3, 256, 128), BF16),
            pltpu.VMEM((8, 256, 128), BF16),
            pltpu.VMEM((8, 256, 128), BF16),
            dma((9,)),
            dma((7,)), dma((7,)),
            dma((8,)), dma((8,)),
            dma((4,)), dma((4,)),
            dma((4,)), dma((4,)),
            dma((7,)), dma((7,)),
            dma((7,)), dma((7,)),
            dma((7,)), dma((7,)),
            dma((8,)),
            dma((7,)), dma((7,)),
            dma((8,)), dma((8,)),
            dma((8,)), dma((8,)),
            dma((8,)), dma((8,)),
        ],
        compiler_params=pltpu.CompilerParams(
            collective_id=0, has_side_effects=True, vmem_limit_bytes=60 * 1024 * 1024
        ),
    )(
        hidden.reshape(256, 4096),
        gain.reshape(1, 4096),
        qkv_w,
        out_w,
        ids.reshape(2, 128),
        embedding[0],
        in_w[0],
        depth_gain,
        depth_qkv[0],
        depth_out[0],
    )
    return temporal.reshape(2, 128, 4096), depth.reshape(2, 128, 1, 1024)


def solution(mesh):
    placed = (
        P(None, "seq", None),
        P(),
        P(None, None, "cb"),
        P("cb", None),
        P(None, "seq", "cb"),
        P("cb", None, None),
        P("cb", "seq", None),
        P("cb", None),
        P("cb", None, None, None),
        P("cb", None, None),
    )
    return jax.shard_map(
        shards,
        mesh=mesh,
        in_specs=placed,
        out_specs=(P(None, "seq", None), P(None, "seq", "cb", None)),
        check_vma=False,
    )
```

time: 420 us -> 141 us (0.34); the launches traced: 414 us -> 141 us
  waiting for transfers between devices: 322 us -> 0 us
  Pallas kernels: 0 us -> 136 us
  matrix products: 33.6 us -> 0 us
  local copies, waits for them, and re-layouts: 29.8 us -> 3.98 us
  other arithmetic: 13.8 us -> 0 us
  between operations: 14.4 us -> 0.65 us
    all_gather x5 -> x0, waiting for transfers between devices: 234 us -> none  [the longest x1 63.3 us: shards(): key_piece = lax.all_gather(book_key[None], 'cb', axis=0, tiled=True)]
    pallas_call x0 -> x1, Pallas kernels: none -> 136 us  [shards(): pl.pallas_call(body, out_shape=(jax.ShapeDtypeStruct((256, 4096), BF16),...]
    psum x1 -> x0, waiting for transfers between devices: 86.9 us -> none  [shards(): summed = lax.psum(term.astype(jnp.bfloat16), 'cb').astype(jnp.float32)]
    dot_general x11 -> x0, matrix products: 33.6 us -> none  [the longest x3 8.17 us: shards(): jnp.dot(normed, temporal_qkv[which], preferred_element_type=jnp.float32)]
    all_gather x2 -> x0, local copies, waits for them, and re-layouts: 13 us -> none  [the longest x1 6.52 us: shards(): value_piece = lax.all_gather(book_value[None], 'cb', axis=0, tiled=True)]
    unnamed x18 -> x4, local copies, waits for them, and re-layouts: 10.6 us -> 3.98 us
    convert_element_type x3 -> x0, other arithmetic: 6.16 us -> none  [the longest x1 3.69 us: shards(): (hidden_f.reshape(row_count, width) + summed).astype(jnp.bfloat16)]
    gather x1 -> x0, local copies, waits for them, and re-layouts: 4.29 us -> none  [shards(): jnp.take(embedding[0], codebook_ids.reshape(row_count), axis=0)]
  transfers between devices with their start and end apart: 6 -> 0, of which waited for: 6 -> 0; matrix products, arithmetic and copies ran while one was open for 9% -> 0% of each run, Pallas kernels for 0% -> 0%
where the time goes in v1:
time: 141 us
  Pallas kernels  136 us (96%)
  local copies, waits for them, and re-layouts  3.98 us (3%)
    pallas_call x1, Pallas kernels, shards(): pl.pallas_call(body, out_shape=(jax.ShapeDtypeStruct((256, 4096), BF16),...  136 us
    unnamed x4, local copies, waits for them, and re-layouts  3.98 us

profile of v1, /device:TPU:126, one launch (start us, length us, event | category | flops | bytes accessed | tf_op | source)
XLA Modules:
  0.0 141.0 jit_solution(7608034529508723277)
XLA Ops:
  0.6 136.4 %shard_map.113 = (bf16[256,4096]{1,0:T(8,128)(2,1)}, bf16[256,1024]{1,0:T(8,128)(2,1)}) custom-call(bf16[256,4096]{1,0:T(8,128)(2,1)} %bitcast.13, f32[1,4096]{1,0:T(1,128)} %bitcast.18, bf16[3,4096,256]{2,1,0:T(8,128)(2,1)} %qkv_w.1, bf16[256,4096]{1,0:T(8,128)(2,1)} %out_w.1, s32[2,128]{1,0:T(2,128)} %bitcast.19, bf16[2048,1024]{1,0:T(8,128)(2,1)} %bitcast.12, ...), custom_call_target="tpu_custom_call" | custom-call | tf_op jit(solution)/shard_map/pallas_call | solution.py:333
  137.1 0.0 copy-start
  137.1 3.2 %copy.15 = bf16[2,128,4096]{2,1,0:T(8,128)(2,1)} copy(bf16[2,128,4096]{2,1,0:T(8,128)(2,1)} %bitcast.15) | data formatting | bytes 4194304
  140.3 0.0 copy-done
  140.3 0.8 copy.16
Async XLA Ops:
  137.1 3.2 %copy-start = (bf16[256,1024]{1,0:T(8,128)(2,1)S(1)}, bf16[256,1024]{1,0:T(8,128)(2,1)}, u32[]{:S(2)}) copy-start(bf16[256,1024]{1,0:T(8,128)(2,1)} %get-tuple-element.5) | copy-start | bytes 1572868

commit v2 on v1

v2 whole, which is shorter than its diff:
```python
import jax
import jax.numpy as jnp
from jax import lax
from jax.experimental import pallas as pl
from jax.experimental.pallas import tpu as pltpu
from jax.sharding import PartitionSpec as P

MESH = pl.DeviceIdType.MESH
F32, BF16 = jnp.float32, jnp.bfloat16
EPS = 1e-05
CB_STEPS = [(0, 1), (0, 3), (0, 2), (1, 0), (1, 1), (1, 3), (1, 2)]
SEQ_STEPS = [(0, 1), (0, 3), (1, 0), (0, 2), (1, 1), (1, 3), (1, 2)]


def dot(a, b):
    return jnp.dot(a, b, preferred_element_type=F32)


def body(
    hidden, gain, qkv_w, out_w, ids, embedding, in_w, depth_gain, depth_qkv, depth_out,
    temporal_out, depth_res,
    hid, normed, wq, kvq, kv, qs, att, mix, wo, tb, win, emb, dw, do, acc, stream, dnorm, dsend, drecv, bsend, brecv,
    local_sem, kv_send, kv_recv, kvf_send, kvf_recv, q_send, q_recv, r_send, r_recv, m_send, m_recv,
    wo_send, wo_recv, wof_send, wof_recv, t_send, t_recv, to_sem, wi_send, wi_recv, wf_send, wf_recv, d_send, d_recv, b_send, b_recv,
):
    s = lax.axis_index("seq")
    c = lax.axis_index("cb")
    yl, x, co = s // 8, (s // 2) % 4, s % 2
    yh, z = c // 4, c % 4
    rank = yl * 2 + co

    def cb_at(step, sign=1):
        return ((yh + step[0]) % 2) * 4 + (z + sign * step[1] + 4) % 4

    def seq_at(step, sign=1):
        return ((yl + step[0]) % 2) * 8 + ((x + sign * step[1] + 4) % 4) * 2 + co

    sibling = s + 1 - 2 * co

    def remote(src, dst, send, recv, device):
        return pltpu.make_async_remote_copy(
            src_ref=src, dst_ref=dst, send_sem=send, recv_sem=recv, device_id=device, device_id_type=MESH
        )

    def arrive(ref, sem):
        pltpu.make_async_copy(ref, ref, sem).wait()

    pending = []

    def send(copy, when=None):
        if when is None:
            copy.start()
        else:
            pl.when(when)(copy.start)
        pending.append((copy, when))

    partner = cb_at((1, 0))
    up, down = cb_at((0, 1)), cb_at((0, 3))

    def lane_send(part, b, sems, row, lane, h, block, to):
        sends, recvs = sems
        ref = part(block, b, h)
        index = 13 * b + 1 + 6 * row + lane
        send(remote(ref, ref, sends.at[index], recvs.at[index], (s, to)))

    def lane_arrive(part, b, sems, row, lane):
        step, h = ((3, 0), (3, 1), (1, 0), (1, 1), (2, 0), (2, 1))[lane]
        arrive(part(cb_at((row, step)), b, h), sems[1].at[13 * b + 1 + 6 * row + lane])

    def along(part, b, sems, row):
        block = partner if row else c
        for lane, h, to in ((0, 0, up), (3, 1, down), (1, 1, up), (2, 0, down)):
            lane_send(part, b, sems, row, lane, h, block, to)

    def spread(part, b, sems):
        own = part(c, b, None)
        send(remote(own, own, sems[0].at[13 * b], sems[1].at[13 * b], (s, partner)))
        along(part, b, sems, 0)

    def pass_on(part, b, sems):
        arrive(part(partner, b, None), sems[1].at[13 * b])
        along(part, b, sems, 1)

    def relay(part, b, sems, row):
        lane_arrive(part, b, sems, row, 0)
        lane_send(part, b, sems, row, 4, 0, cb_at((row, 3)), up)
        lane_arrive(part, b, sems, row, 3)
        lane_send(part, b, sems, row, 5, 1, cb_at((row, 1)), down)

    def arrivals(part, b, sems):
        yield partner
        for row in range(2):
            for lane, step in ((1, 3), (2, 1)):
                lane_arrive(part, b, sems, row, lane)
                yield cb_at((row, step))
        for row in range(2):
            for lane in (4, 5):
                lane_arrive(part, b, sems, row, lane)
            yield cb_at((row, 2))

    def forward(part, sems):
        pass_on(part, 0, sems)
        relay(part, 0, sems, 0)
        pass_on(part, 1, sems)
        relay(part, 1, sems, 0)
        relay(part, 0, sems, 1)
        relay(part, 1, sems, 1)

    def mix_part(group, b, h):
        return mix.at[group, pl.ds(2 * b, 2) if h is None else 2 * b + h]

    def tb_part(group, b, h):
        return tb.at[group, pl.ds(128 * b, 128) if h is None else pl.ds(128 * b + 64 * h, 64)]

    mix_sems, tb_sems = (m_send, m_recv), (t_send, t_recv)

    across = seq_at((1, 0))
    right, left = seq_at((0, 1)), seq_at((0, 3))

    def in_half(block, h):
        return win.at[block, pl.ds(128 * h, 128)]

    def in_send(row, lane, ref, source, to):
        send(remote(source, ref, wi_send.at[1 + 6 * row + lane], wi_recv.at[1 + 6 * row + lane], (to, c)))

    def in_arrive(row, lane):
        step, h = ((3, 0), (3, 1), (1, 0), (1, 1), (2, 0), (2, 1))[lane]
        arrive(in_half(seq_at((row, step)), h), wi_recv.at[1 + 6 * row + lane])

    def in_relay(row):
        in_arrive(row, 0)
        ref = in_half(seq_at((row, 3)), 0)
        in_send(row, 4, ref, ref, right)
        in_arrive(row, 3)
        ref = in_half(seq_at((row, 1)), 1)
        in_send(row, 5, ref, ref, left)

    def in_share(block, index):
        send(remote(win.at[block], win.at[block], wf_send.at[index], wf_recv.at[index], (sibling, c)))

    barrier = pltpu.get_barrier_semaphore()
    for step in CB_STEPS:
        pl.semaphore_signal(barrier, inc=1, device_id=(s, cb_at(step)), device_id_type=MESH)
    for step in SEQ_STEPS:
        pl.semaphore_signal(barrier, inc=1, device_id=(seq_at(step), c), device_id_type=MESH)
        other = seq_at(step) + 1 - 2 * co
        pl.semaphore_signal(barrier, inc=1, device_id=(other, c), device_id_type=MESH)
    pl.semaphore_signal(barrier, inc=1, device_id=(sibling, c), device_id_type=MESH)

    loads = [
        pltpu.make_async_copy(hidden, hid, local_sem.at[0]),
        pltpu.make_async_copy(qkv_w.at[1], wq.at[1], local_sem.at[1]),
        pltpu.make_async_copy(qkv_w.at[2], wq.at[2], local_sem.at[2]),
        pltpu.make_async_copy(qkv_w.at[0], wq.at[0], local_sem.at[3]),
        pltpu.make_async_copy(out_w.at[:, pl.ds(pl.multiple_of(c * 512, 512), 512)], wo.at[c], local_sem.at[4]),
        pltpu.make_async_copy(in_w, win.at[s], local_sem.at[5]),
        pltpu.make_async_copy(embedding, emb, local_sem.at[6]),
        pltpu.make_async_copy(depth_qkv, dw, local_sem.at[7]),
        pltpu.make_async_copy(depth_out, do, local_sem.at[8]),
    ]
    for copy in loads:
        copy.start()

    loads[0].wait()

    @pl.loop(0, 16)
    def _(i):
        rows = pl.ds(pl.multiple_of(i * 16, 16), 16)
        values = hid[rows, :].astype(F32)
        mean_sq = jnp.mean(values * values, axis=-1, keepdims=True)
        normed[rows, :] = (values * lax.rsqrt(mean_sq + EPS) * gain[...]).astype(BF16)

    def project(which, slot):
        loads[{1: 1, 2: 2, 0: 3}[which]].wait()
        res = dot(normed[...], wq[which]).astype(BF16)
        for g in range(4):
            b, h = g // 2, g % 2
            kvq[g, slot] = res[b * 128 : (b + 1) * 128, h * 128 : (h + 1) * 128]

    pl.semaphore_wait(barrier, 22)
    half = pl.ds(pl.multiple_of(co * 128, 128), 128)
    for i, step in enumerate(CB_STEPS):
        to = cb_at(step)
        columns = pl.ds(pl.multiple_of(to * 512, 512), 512)
        send(remote(out_w.at[half, columns], wo.at[c, half], wo_send.at[i], wo_recv.at[i], (s, to)))
    in_send(0, 0, in_half(s, 0), in_w.at[pl.ds(0, 128)], right)
    in_send(0, 3, in_half(s, 1), in_w.at[pl.ds(128, 128)], left)

    project(1, 0)
    project(2, 1)

    for i, step in enumerate(SEQ_STEPS):
        to = seq_at(step)
        g = (to // 2) % 4
        send(remote(kvq.at[g, pl.ds(0, 2)], kv.at[s], kv_send.at[i], kv_recv.at[i], (to, c)))
    kv[s] = kvq[x, 0:2]
    send(remote(kv.at[s], kv.at[s], kvf_send.at[7], kvf_recv.at[7], (sibling, c)))

    project(0, 2)
    turn = s % 8
    owner = jnp.where(turn < 4, turn, 7 - turn)
    strip = s // 4
    for dx in range(4):
        g = (x + dx) % 4
        to = (owner // 2) * 8 + g * 2 + owner % 2
        copy = remote(kvq.at[g, 2], qs.at[strip], q_send.at[dx], q_recv.at[strip], (to, c))
        send(copy, None if dx else owner != rank)

    @pl.when(owner == rank)
    def _():
        qs[strip] = kvq[x, 2]

    send(remote(in_w, win.at[s], wi_send.at[0], wi_recv.at[0], (across, c)))
    in_send(0, 1, in_half(s, 1), in_w.at[pl.ds(128, 128)], right)
    in_send(0, 2, in_half(s, 0), in_w.at[pl.ds(0, 128)], left)
    send(remote(in_w, win.at[s], wf_send.at[0], wf_recv.at[0], (sibling, c)))
    in_relay(0)
    for i, step in enumerate(CB_STEPS):
        group = cb_at(step, -1)
        arrive(wo.at[group, half], wo_recv.at[i])
        send(remote(wo.at[group, half], wo.at[group, half], wof_send.at[i], wof_recv.at[i], (sibling, c)))

    for i, step in enumerate(SEQ_STEPS):
        source = seq_at(step, -1)
        arrive(kv.at[source], kv_recv.at[i])
        send(remote(kv.at[source], kv.at[source], kvf_send.at[i], kvf_recv.at[i], (sibling, c)))
    arrive(kv.at[sibling], kvf_recv.at[7])
    for i, step in enumerate(SEQ_STEPS):
        source = seq_at(step, -1) + 1 - 2 * co
        arrive(kv.at[source], kvf_recv.at[i])

    for k in range(4):
        block = 4 * k + (rank if k % 2 == 0 else 3 - rank)

        @pl.when(block != s)
        def _():
            arrive(qs.at[k], q_recv.at[k])

        n = 4 * (k + 1)
        keys = kv[0:n, 0].reshape(n * 128, 128)
        values = kv[0:n, 1].reshape(n * 128, 128)
        scores = lax.dot_general(qs[k], keys, (((1,), (1,)), ((), ())), preferred_element_type=F32)
        row = lax.broadcasted_iota(jnp.int32, scores.shape, 0) + block * 128
        col = lax.broadcasted_iota(jnp.int32, scores.shape, 1)
        allowed = col <= row
        scores = jnp.where(allowed, scores * (128.0**-0.5), -1e30)
        weights = jnp.where(allowed, jnp.exp(scores - jnp.max(scores, axis=-1, keepdims=True)), 0.0)
        totals = jnp.sum(weights, axis=-1, keepdims=True)
        att[k] = (dot(weights.astype(BF16), values) / totals).astype(BF16)
        send(remote(att.at[k], mix.at[c, x], r_send.at[k], r_recv.at[x], (block, c)), block != s)

        @pl.when(block == s)
        def _():
            mix[c, x] = att[k]

    for b in range(2):
        for g in (2 * b, 2 * b + 1):
            @pl.when(jnp.logical_or(g != x, owner != rank))
            def _():
                arrive(mix.at[c, g], r_recv.at[g])

        spread(mix_part, b, mix_sems)

    arrive(win.at[across], wi_recv.at[0])
    for lane, h, to in ((0, 0, right), (3, 1, left), (1, 1, right), (2, 0, left)):
        in_send(1, lane, in_half(across, h), in_half(across, h), to)
    forward(mix_part, mix_sems)

    loads[6].wait()
    picks = []
    for b in range(2):
        picks.append(jnp.broadcast_to(ids[b : b + 1, :], (128, 128)).T)
    acc[...] = jnp.zeros_like(acc)

    @pl.loop(0, 8)
    def _(k):
        lane = lax.broadcasted_iota(jnp.int32, (128, 128), 1) + k * 256
        hot = [
            jnp.concatenate([jnp.where(pick == lane + 128 * j, 1.0, 0.0).astype(BF16) for j in range(2)], axis=1)
            for pick in picks
        ]
        acc[...] += dot(jnp.concatenate(hot, axis=0), emb[pl.ds(pl.multiple_of(k * 256, 256), 256), :])
    loads[5].wait()
    for lane in (1, 2, 4, 5):
        in_arrive(0, lane)
    for i in (1, 3, 2):
        in_share(seq_at((0, i)), 1 + i)

    def group_term(group, b):
        return dot(jnp.concatenate([mix[group, 2 * b], mix[group, 2 * b + 1]], axis=1), wo[group])

    loads[4].wait()
    other_half = pl.ds(pl.multiple_of(128 - co * 128, 128), 128)
    for i, step in enumerate(CB_STEPS):
        arrive(wo.at[cb_at(step, -1), other_half], wof_recv.at[i])
    mine = pl.ds(pl.multiple_of(c * 512, 512), 512)
    for b in range(2):
        summed = group_term(c, b)
        for group in arrivals(mix_part, b, mix_sems):
            summed = summed + group_term(group, b)
        rows = pl.ds(128 * b, 128)
        tb[c, rows, :] = (hid[rows, mine].astype(F32) + summed).astype(BF16)
        spread(tb_part, b, tb_sems)
    stores = []

    def store(index, group):
        columns = pl.ds(pl.multiple_of(group * 512, 512), 512)
        copy = pltpu.make_async_copy(tb.at[group], temporal_out.at[:, columns], to_sem.at[index])
        copy.start()
        stores.append(copy)

    store(7, c)

    in_relay(1)
    in_share(across, 1)
    forward(tb_part, tb_sems)
    for lane in (1, 2, 4, 5):
        in_arrive(1, lane)
    for i in (1, 3, 2):
        in_share(seq_at((1, i)), 4 + i)
    twin = 1 - 2 * co
    arrive(win.at[sibling], wf_recv.at[0])
    arrive(win.at[across + twin], wf_recv.at[1])
    for row in range(2):
        for i in (1, 3, 2):
            arrive(win.at[seq_at((row, i)) + twin], wf_recv.at[1 + 3 * row + i])

    loads[7].wait()
    for b in range(2):
        half_rows = pl.ds(128 * b, 128)

        def add_block(group):
            rows = jnp.concatenate([win[2 * group], win[2 * group + 1]], axis=0)
            acc[half_rows, :] += dot(tb[group, half_rows, :], rows)

        add_block(c)
        for i, group in enumerate(arrivals(tb_part, b, tb_sems)):
            if b:
                store(i, group)
            add_block(group)

        @pl.loop(0, 4)
        def _(i):
            rows = pl.ds(pl.multiple_of(i * 32 + 128 * b, 32), 32)
            rounded = acc[rows, :].astype(BF16)
            stream[rows, :] = rounded
            values = rounded.astype(F32)
            mean_sq = jnp.mean(values * values, axis=-1, keepdims=True)
            dnorm[rows, :] = (values * lax.rsqrt(mean_sq + EPS) * depth_gain[...]).astype(BF16)

        for i in (2, 1, 3, 0):
            pair = (c // 2 + i) % 4
            columns = pl.ds(pl.multiple_of(pair * 256, 256), 256)
            for which in range(3):
                res = dot(dnorm[half_rows, :], dw[which, :, columns]).astype(BF16)
                dsend[b, 2 * pair, which] = res[:, 0:128]
                dsend[b, 2 * pair + 1, which] = res[:, 128:256]
            if i:
                for j in range(2):
                    to = 2 * pair + j
                    send(remote(dsend.at[b, to], drecv.at[b, c], d_send.at[8 * b + 2 * i + j], d_recv.at[8 * b + c], (s, to)))
            else:
                to = c + 1 - 2 * (c % 2)
                send(remote(dsend.at[b, to], drecv.at[b, c], d_send.at[8 * b], d_recv.at[8 * b + c], (s, to)))
                drecv[b, c] = dsend[b, c]

    half_a = lax.broadcasted_iota(jnp.int32, (256, 128), 0) % 128 // 64
    half_b = lax.broadcasted_iota(jnp.int32, (256, 128), 1) // 64
    same_head = jnp.where(half_a == half_b, 1.0, 0.0).astype(BF16)
    size = 64
    for b in range(2):
        for book in range(8):
            @pl.when(book != c)
            def _():
                arrive(drecv.at[b, book], d_recv.at[8 * b + book])

        for book in range(8):
            @pl.loop(0, 128 // size)
            def _(i):
                rows = pl.ds(pl.multiple_of(i * size, size), size)
                query = drecv[b, book, 0, rows, :].astype(F32)
                parts = []
                for j in range(book + 1):
                    prod = query * drecv[b, j, 1, rows, :].astype(F32)
                    high = prod.astype(BF16)
                    low = (prod - high.astype(F32)).astype(BF16)
                    parts.append(jnp.concatenate([high, low], axis=1))
                scores = dot(jnp.concatenate(parts, axis=0), same_head)
                scores = [scores[j * size : (j + 1) * size] for j in range(book + 1)]
                highest = scores[0]
                for j in range(1, book + 1):
                    highest = jnp.maximum(highest, scores[j])
                totals = jnp.zeros((size, 128), F32)
                mixed = jnp.zeros((size, 128), F32)
                for j in range(book + 1):
                    weight = jnp.exp((scores[j] - highest) * 0.125)
                    totals = totals + weight
                    mixed = mixed + weight.astype(BF16).astype(F32) * drecv[b, j, 2, rows, :].astype(F32)
                bsend[b, book, rows, :] = (mixed / totals).astype(BF16)

            send(remote(bsend.at[b, book], brecv.at[b, c], b_send.at[8 * b + book], b_recv.at[8 * b + c], (s, book)), book != c)

            @pl.when(book == c)
            def _():
                brecv[b, c] = bsend[b, book]

    loads[8].wait()
    for b in range(2):
        for head in range(8):
            @pl.when(head != c)
            def _():
                arrive(brecv.at[b, head], b_recv.at[8 * b + head])

        book_mixed = jnp.concatenate([brecv[b, head] for head in range(8)], axis=1)
        rows = pl.ds(128 * b, 128)
        depth_res[rows, :] = (dot(book_mixed, do[...]) + stream[rows, :].astype(F32)).astype(BF16)

    for copy in stores:
        copy.wait()
    for copy, when in pending:
        if when is None:
            copy.wait_send()
        else:
            pl.when(when)(copy.wait_send)


def shards(hidden, gain, qkv_w, out_w, ids, embedding, in_w, depth_gain, depth_qkv, depth_out):
    anywhere = pl.BlockSpec(memory_space=pl.ANY)
    hbm = pl.BlockSpec(memory_space=pltpu.HBM)
    vmem = pl.BlockSpec(memory_space=pltpu.VMEM)
    dma = pltpu.SemaphoreType.DMA
    temporal, depth = pl.pallas_call(
        body,
        out_shape=(jax.ShapeDtypeStruct((256, 4096), BF16), jax.ShapeDtypeStruct((256, 1024), BF16)),
        in_specs=[hbm, vmem, hbm, hbm, vmem, hbm, hbm, vmem, hbm, hbm],
        out_specs=(anywhere, vmem),
        scratch_shapes=[
            pltpu.VMEM((256, 4096), BF16),
            pltpu.VMEM((256, 4096), BF16),
            pltpu.VMEM((3, 4096, 256), BF16),
            pltpu.VMEM((4, 3, 128, 128), BF16),
            pltpu.VMEM((16, 2, 128, 128), BF16),
            pltpu.VMEM((4, 128, 128), BF16),
            pltpu.VMEM((4, 128, 128), BF16),
            pltpu.VMEM((8, 4, 128, 128), BF16),
            pltpu.VMEM((8, 256, 512), BF16),
            pltpu.VMEM((8, 256, 512), BF16),
            pltpu.VMEM((16, 256, 1024), BF16),
            pltpu.VMEM((2048, 1024), BF16),
            pltpu.VMEM((3, 1024, 1024), BF16),
            pltpu.VMEM((1024, 1024), BF16),
            pltpu.VMEM((256, 1024), F32),
            pltpu.VMEM((256, 1024), BF16),
            pltpu.VMEM((256, 1024), BF16),
            pltpu.VMEM((2, 8, 3, 128, 128), BF16),
            pltpu.VMEM((2, 8, 3, 128, 128), BF16),
            pltpu.VMEM((2, 8, 128, 128), BF16),
            pltpu.VMEM((2, 8, 128, 128), BF16),
            dma((9,)),
            dma((7,)), dma((7,)),
            dma((8,)), dma((8,)),
            dma((4,)), dma((4,)),
            dma((4,)), dma((4,)),
            dma((26,)), dma((26,)),
            dma((7,)), dma((7,)),
            dma((7,)), dma((7,)),
            dma((26,)), dma((26,)),
            dma((8,)),
            dma((13,)), dma((13,)),
            dma((8,)), dma((8,)),
            dma((16,)), dma((16,)),
            dma((16,)), dma((16,)),
        ],
        compiler_params=pltpu.CompilerParams(
            collective_id=0, has_side_effects=True, vmem_limit_bytes=48 * 1024 * 1024
        ),
    )(
        hidden.reshape(256, 4096),
        gain.reshape(1, 4096),
        qkv_w,
        out_w,
        ids.reshape(2, 128),
        embedding[0],
        in_w[0],
        depth_gain,
        depth_qkv[0],
        depth_out[0],
    )
    return temporal.reshape(2, 128, 4096), depth.reshape(2, 128, 1, 1024)


def solution(mesh):
    placed = (
        P(None, "seq", None),
        P(),
        P(None, None, "cb"),
        P("cb", None),
        P(None, "seq", "cb"),
        P("cb", None, None),
        P("cb", "seq", None),
        P("cb", None),
        P("cb", None, None, None),
        P("cb", None, None),
    )
    return jax.shard_map(
        shards,
        mesh=mesh,
        in_specs=placed,
        out_specs=(P(None, "seq", None), P(None, "seq", "cb", None)),
        check_vma=False,
    )
```

time: 141 us -> 112 us (0.79); the launches traced: 141 us -> 110 us
  Pallas kernels: 136 us -> 102 us
  local copies, waits for them, and re-layouts: 3.98 us -> 6.82 us
    pallas_call x1, Pallas kernels: 136 us -> 102 us  [shards(): pl.pallas_call(body, out_shape=(jax.ShapeDtypeStruct((256, 4096), BF16),...]
    unnamed x4 -> x12, local copies, waits for them, and re-layouts: 3.98 us -> 6.82 us
where the time goes in v2:
time: 112 us; the launch traced here: 110 us
  Pallas kernels  102 us (91%)
  local copies, waits for them, and re-layouts  6.82 us (6%)
    pallas_call x1, Pallas kernels, shards(): pl.pallas_call(body, out_shape=(jax.ShapeDtypeStruct((256, 4096), BF16),...  102 us
    unnamed x12, local copies, waits for them, and re-layouts  6.82 us

profile of v2, /device:TPU:126, one launch (start us, length us, event | category | flops | bytes accessed | tf_op | source)
XLA Modules:
  0.0 109.7 jit_solution(15807494563050070221)
XLA Ops:
  0.6 0.0 copy-start
  0.6 1.6 %copy-done = bf16[2,128,4096]{2,1,0:T(8,128)(2,1)S(1)} copy-done((bf16[2,128,4096]{2,1,0:T(8,128)(2,1)S(1)}, bf16[2,128,4096]{2,1,0:T(8,128)(2,1)}, u32[]{:S(2)}) %copy-start) | copy-done | bytes 2097176
  2.2 0.0 copy-start.1
  2.2 1.0 copy-done.1
  3.3 0.0 copy-start.2
  3.3 0.7 copy-done.2
  4.0 0.0 copy-start.3
  4.0 0.7 copy-done.3
  4.7 0.0 copy-start.4
  4.7 0.7 copy-done.4
  5.4 102.2 %shard_map.113 = (bf16[256,4096]{1,0:T(8,128)(2,1)S(1)}, bf16[256,1024]{1,0:T(8,128)(2,1)S(1)}) custom-call(bf16[256,4096]{1,0:T(8,128)(2,1)S(1)} %bitcast.11, f32[1,4096]{1,0:T(1,128)S(1)} %bitcast.15, bf16[3,4096,256]{2,1,0:T(8,128)(2,1)} %qkv_w.1, bf16[256,4096]{1,0:T(8,128)(2,1)} %out_w.1, s32[2,128]{1,0:T(2,128)S(1)} %bitcast.16, ...), custom_call_target="tpu_custom_call" | custom-call | tf_op jit(solution)/shard_map/pallas_call | solution.py:432
  107.6 1.3 %copy.15 = bf16[2,128,4096]{2,1,0:T(8,128)(2,1)} copy(bf16[2,128,4096]{2,1,0:T(8,128)(2,1)S(1)} %bitcast.12) | data formatting | bytes 4194304
  108.9 0.8 copy.16
Async XLA Ops:
  0.6 1.6 %copy-start = (bf16[2,128,4096]{2,1,0:T(8,128)(2,1)S(1)}, bf16[2,128,4096]{2,1,0:T(8,128)(2,1)}, u32[]{:S(2)}) copy-start(bf16[2,128,4096]{2,1,0:T(8,128)(2,1)} %param.10) | copy-start | bytes 6291460
  2.2 1.0 copy-start.1
  3.3 0.7 copy-start.2
  4.0 0.7 copy-start.3
  4.7 0.7 copy-start.4

commit v3 on v2

--- a/solution.py
+++ b/solution.py
@@ -19,7 +19,7 @@
 def body(
     hidden, gain, qkv_w, out_w, ids, embedding, in_w, depth_gain, depth_qkv, depth_out,
     temporal_out, depth_res,
-    hid, normed, wq, kvq, kv, qs, att, mix, wo, tb, win, emb, dw, do, acc, stream, dnorm, dsend, drecv, bsend, brecv,
+    normed, wq, kvq, kv, qs, att, mix, wo, tb, win, emb, dw, do, acc, stream, dnorm, dsend, drecv, bsend, brecv,
     local_sem, kv_send, kv_recv, kvf_send, kvf_recv, q_send, q_recv, r_send, r_recv, m_send, m_recv,
     wo_send, wo_recv, wof_send, wof_recv, t_send, t_recv, to_sem, wi_send, wi_recv, wf_send, wf_recv, d_send, d_recv, b_send, b_recv,
 ):
@@ -148,25 +148,24 @@
     pl.semaphore_signal(barrier, inc=1, device_id=(sibling, c), device_id_type=MESH)
 
     loads = [
-        pltpu.make_async_copy(hidden, hid, local_sem.at[0]),
+        pltpu.make_async_copy(in_w, win.at[s], local_sem.at[0]),
         pltpu.make_async_copy(qkv_w.at[1], wq.at[1], local_sem.at[1]),
         pltpu.make_async_copy(qkv_w.at[2], wq.at[2], local_sem.at[2]),
         pltpu.make_async_copy(qkv_w.at[0], wq.at[0], local_sem.at[3]),
         pltpu.make_async_copy(out_w.at[:, pl.ds(pl.multiple_of(c * 512, 512), 512)], wo.at[c], local_sem.at[4]),
-        pltpu.make_async_copy(in_w, win.at[s], local_sem.at[5]),
+        None,
         pltpu.make_async_copy(embedding, emb, local_sem.at[6]),
         pltpu.make_async_copy(depth_qkv, dw, local_sem.at[7]),
         pltpu.make_async_copy(depth_out, do, local_sem.at[8]),
     ]
     for copy in loads:
-        copy.start()
-
-    loads[0].wait()
+        if copy is not None:
+            copy.start()
 
     @pl.loop(0, 16)
     def _(i):
         rows = pl.ds(pl.multiple_of(i * 16, 16), 16)
-        values = hid[rows, :].astype(F32)
+        values = hidden[rows, :].astype(F32)
         mean_sq = jnp.mean(values * values, axis=-1, keepdims=True)
         normed[rows, :] = (values * lax.rsqrt(mean_sq + EPS) * gain[...]).astype(BF16)
 
@@ -219,6 +218,21 @@
         group = cb_at(step, -1)
         arrive(wo.at[group, half], wo_recv.at[i])
         send(remote(wo.at[group, half], wo.at[group, half], wof_send.at[i], wof_recv.at[i], (sibling, c)))
+
+    loads[6].wait()
+    picks = []
+    for b in range(2):
+        picks.append(jnp.broadcast_to(ids[b : b + 1, :], (128, 128)).T)
+    acc[...] = jnp.zeros_like(acc)
+
+    @pl.loop(0, 8)
+    def _(k):
+        lane = lax.broadcasted_iota(jnp.int32, (128, 128), 1) + k * 256
+        hot = [
+            jnp.concatenate([jnp.where(pick == lane + 128 * j, 1.0, 0.0).astype(BF16) for j in range(2)], axis=1)
+            for pick in picks
+        ]
+        acc[...] += dot(jnp.concatenate(hot, axis=0), emb[pl.ds(pl.multiple_of(k * 256, 256), 256), :])
 
     for i, step in enumerate(SEQ_STEPS):
         source = seq_at(step, -1)
@@ -266,21 +280,7 @@
         in_send(1, lane, in_half(across, h), in_half(across, h), to)
     forward(mix_part, mix_sems)
 
-    loads[6].wait()
-    picks = []
-    for b in range(2):
-        picks.append(jnp.broadcast_to(ids[b : b + 1, :], (128, 128)).T)
-    acc[...] = jnp.zeros_like(acc)
-
-    @pl.loop(0, 8)
-    def _(k):
-        lane = lax.broadcasted_iota(jnp.int32, (128, 128), 1) + k * 256
-        hot = [
-            jnp.concatenate([jnp.where(pick == lane + 128 * j, 1.0, 0.0).astype(BF16) for j in range(2)], axis=1)
-            for pick in picks
-        ]
-        acc[...] += dot(jnp.concatenate(hot, axis=0), emb[pl.ds(pl.multiple_of(k * 256, 256), 256), :])
-    loads[5].wait()
+    loads[0].wait()
     for lane in (1, 2, 4, 5):
         in_arrive(0, lane)
     for i in (1, 3, 2):
@@ -299,7 +299,7 @@
         for group in arrivals(mix_part, b, mix_sems):
             summed = summed + group_term(group, b)
         rows = pl.ds(128 * b, 128)
-        tb[c, rows, :] = (hid[rows, mine].astype(F32) + summed).astype(BF16)
+        tb[c, rows, :] = (hidden[rows, mine].astype(F32) + summed).astype(BF16)
         spread(tb_part, b, tb_sems)
     stores = []
 
@@ -313,7 +313,11 @@
 
     in_relay(1)
     in_share(across, 1)
-    forward(tb_part, tb_sems)
+    pass_on(tb_part, 0, tb_sems)
+    relay(tb_part, 0, tb_sems, 0)
+    pass_on(tb_part, 1, tb_sems)
+    relay(tb_part, 1, tb_sems, 0)
+    relay(tb_part, 0, tb_sems, 1)
     for lane in (1, 2, 4, 5):
         in_arrive(1, lane)
     for i in (1, 3, 2):
@@ -348,6 +352,8 @@
             mean_sq = jnp.mean(values * values, axis=-1, keepdims=True)
             dnorm[rows, :] = (values * lax.rsqrt(mean_sq + EPS) * depth_gain[...]).astype(BF16)
 
+        if b == 0:
+            relay(tb_part, 1, tb_sems, 1)
         for i in (2, 1, 3, 0):
             pair = (c // 2 + i) % 4
             columns = pl.ds(pl.multiple_of(pair * 256, 256), 256)
@@ -432,10 +438,9 @@
     temporal, depth = pl.pallas_call(
         body,
         out_shape=(jax.ShapeDtypeStruct((256, 4096), BF16), jax.ShapeDtypeStruct((256, 1024), BF16)),
-        in_specs=[hbm, vmem, hbm, hbm, vmem, hbm, hbm, vmem, hbm, hbm],
+        in_specs=[vmem, vmem, hbm, hbm, vmem, hbm, hbm, vmem, hbm, hbm],
         out_specs=(anywhere, vmem),
         scratch_shapes=[
-            pltpu.VMEM((256, 4096), BF16),
             pltpu.VMEM((256, 4096), BF16),
             pltpu.VMEM((3, 4096, 256), BF16),
             pltpu.VMEM((4, 3, 128, 128), BF16),

time: 112 us -> 110 us (0.982)
    pallas_call x1, Pallas kernels: 102 us -> 101 us  [shards(): pl.pallas_call(body, out_shape=(jax.ShapeDtypeStruct((256, 4096), BF16),...]
where the time goes in v3:
time: 110 us; the launch traced here: 108 us
  Pallas kernels  101 us (92%)
  local copies, waits for them, and re-layouts  6.82 us (6%)
    pallas_call x1, Pallas kernels, shards(): pl.pallas_call(body, out_shape=(jax.ShapeDtypeStruct((256, 4096), BF16),...  101 us
    unnamed x12, local copies, waits for them, and re-layouts  6.82 us

profile of v3, /device:TPU:126, one launch (start us, length us, event | category | flops | bytes accessed | tf_op | source)
XLA Modules:
  0.0 108.1 jit_solution(4366619213821076914)
XLA Ops:
  0.6 0.0 copy-start
  0.6 1.6 %copy-done = bf16[2,128,4096]{2,1,0:T(8,128)(2,1)S(1)} copy-done((bf16[2,128,4096]{2,1,0:T(8,128)(2,1)S(1)}, bf16[2,128,4096]{2,1,0:T(8,128)(2,1)}, u32[]{:S(2)}) %copy-start) | copy-done | bytes 2097176
  2.2 0.0 copy-start.1
  2.2 1.0 copy-done.1
  3.3 0.0 copy-start.2
  3.3 0.7 copy-done.2
  4.0 0.0 copy-start.3
  4.0 0.7 copy-done.3
  4.7 0.0 copy-start.4
  4.7 0.7 copy-done.4
  5.4 100.7 %shard_map.113 = (bf16[256,4096]{1,0:T(8,128)(2,1)S(1)}, bf16[256,1024]{1,0:T(8,128)(2,1)S(1)}) custom-call(bf16[256,4096]{1,0:T(8,128)(2,1)S(1)} %bitcast.11, f32[1,4096]{1,0:T(1,128)S(1)} %bitcast.15, bf16[3,4096,256]{2,1,0:T(8,128)(2,1)} %qkv_w.1, bf16[256,4096]{1,0:T(8,128)(2,1)} %out_w.1, s32[2,128]{1,0:T(2,128)S(1)} %bitcast.16, ...), custom_call_target="tpu_custom_call" | custom-call | tf_op jit(solution)/shard_map/pallas_call | solution.py:438
  106.0 1.3 %copy.15 = bf16[2,128,4096]{2,1,0:T(8,128)(2,1)} copy(bf16[2,128,4096]{2,1,0:T(8,128)(2,1)S(1)} %bitcast.12) | data formatting | bytes 4194304
  107.3 0.8 copy.16
Async XLA Ops:
  0.6 1.6 %copy-start = (bf16[2,128,4096]{2,1,0:T(8,128)(2,1)S(1)}, bf16[2,128,4096]{2,1,0:T(8,128)(2,1)}, u32[]{:S(2)}) copy-start(bf16[2,128,4096]{2,1,0:T(8,128)(2,1)} %param.10) | copy-start | bytes 6291460
  2.2 1.0 copy-start.1
  3.3 0.7 copy-start.2
  4.0 0.7 copy-start.3
  4.7 0.7 copy-start.4
